TPU v7x, 32 devices: a whole 2x2x4 slice. The times are simulated.
32 devices in a mesh: dp: 8 (over y, x, core), mp: 4 (over z).
Axes of the slice: x: 2, y: 2, z: 4, core: 2. Of those that a mesh axis runs over, the one named last changes fastest.
Arguments:
- hidden: bfloat16 [4096, 768], P('dp'), may hold values from -6 to 6
- memory: bfloat16 [32768, 768], P('dp', 'mp'), may hold values from -6 to 6
- out_grad: bfloat16 [4096, 768], P('dp'), may hold values from -6 to 6
- dec_starts: int32 [32, 4], P('dp'), may hold values from 0 to 127, as said below
- dec_length: int32 [32], P('dp'), may hold values from 96 to 128
- mem_starts: int32 [32, 4], P('dp'), may hold values from 0 to 1023, as said below
- mem_length: int32 [32], P('dp'), may hold values from 768 to 1024
- self_qkv: bfloat16 [3, 768, 768], P(None, None, 'mp'), may hold values from -0.25 to 0.25
- self_qv_bias: float32 [2, 768], P(None, 'mp'), may hold values from -3 to 3
- self_proj: bfloat16 [768, 768], P('mp'), may hold values from -0.3125 to 0.3125
- cross_query: bfloat16 [768, 768], P(None, 'mp'), may hold values from -0.25 to 0.25
- cross_kv: bfloat16 [2, 768, 768], P(None, None, 'mp'), may hold values from -0.25 to 0.25
- cross_qv_bias: float32 [2, 768], P(None, 'mp'), may hold values from -3 to 3
- cross_proj: bfloat16 [768, 768], P('mp'), may hold values from -0.875 to 0.875
- ffn_in: bfloat16 [768, 3072], P(None, 'mp'), may hold values from -0.21875 to 0.21875
- ffn_in_bias: float32 [3072], P('mp'), may hold values from -3 to 3
- ffn_out: bfloat16 [3072, 768], P('mp'), may hold values from -0.15625 to 0.15625
- out_biases: float32 [3, 768], replicated, may hold values from -3 to 3
- norm_gains: float32 [3, 768], replicated, may hold values from 0.25 to 1.75
- norm_biases: float32 [3, 768], replicated, may hold values from -2 to 2
Outputs:
- result: bfloat16 [4096, 768], P('dp')
- hidden_grad: float32 [4096, 768], P('dp')
- memory_grad: float32 [32768, 768], P('dp', 'mp')
- self_qkv_grad: float32 [3, 768, 768], P(None, None, 'mp')
- self_qv_bias_grad: float32 [2, 768], P(None, 'mp')
- self_proj_grad: float32 [768, 768], P('mp')
- cross_query_grad: float32 [768, 768], P(None, 'mp')
- cross_kv_grad: float32 [2, 768, 768], P(None, None, 'mp')
- cross_qv_bias_grad: float32 [2, 768], P(None, 'mp')
- cross_proj_grad: float32 [768, 768], P('mp')
- ffn_in_grad: float32 [768, 3072], P(None, 'mp')
- ffn_in_bias_grad: float32 [3072], P('mp')
- ffn_out_grad: float32 [3072, 768], P('mp')
- out_biases_grad: float32 [3, 768], replicated
- norm_gains_grad: float32 [3, 768], replicated
- norm_biases_grad: float32 [3, 768], replicated
Inputs may be any that keep to these rules, and one draw needn't show every extreme that they name: `dec_starts`: each packed row holds 4 pairs; its offsets start at 0, rise strictly and stay below the row's used slots, so every decoder segment holds at least one used slot; padded slots belong to the last pair. `mem_starts`: pair j's table is memory segment j of the same packed row; offsets start at 0, rise strictly and stay below the row's used slots, so every memory segment holds at least one used slot.
All inputs are finite; a program needn't handle non-finite values.
Results may differ from a plain program's by a relative error of at most 0.023.
Values may be sent and summed in bfloat16 or wider, within the bound.
No kernel may reach another device: no remote copies, remote signals or barrier semaphores. Data moves between devices by JAX's collectives and lax.ppermute only.
A program may use at most 128 MiB of HBM per device.

v0:
```python
import jax
import jax.numpy as jnp
from jax import lax
from jax.sharding import PartitionSpec as P

HD = 64
NEG_FILL = -1000000000.0
EPSILON = 1e-05


def layer_norm(values, gain_row, bias_row):
    average = jnp.mean(values, -1, keepdims=True)
    centered = values - average
    variance = jnp.mean(centered * centered, -1, keepdims=True)
    return centered * lax.rsqrt(variance + EPSILON) * gain_row + bias_row


def exact_gelu(values):
    return jax.nn.gelu(values, approximate=False)


def segment_ids(starts, slot_count):
    places = jnp.arange(slot_count, dtype=jnp.int32)
    return jnp.sum((starts[:, None, :] <= places[None, :, None]).astype(jnp.int32), -1) - 1


def inner_dot(left_side, right_side):
    return lax.dot_general(
        left_side, right_side, (((0,), (0,)), ((), ())), preferred_element_type=jnp.float32
    )


def outer_dot(left_side, right_side):
    return lax.dot_general(
        left_side, right_side, (((1,), (1,)), ((), ())), preferred_element_type=jnp.float32
    )


def row_groups(kernel, arrays):
    row_count = arrays[0].shape[0]
    limit = max(1, 512 // arrays[0].shape[1])
    group_rows = max(
        (count for count in range(1, min(row_count, limit) + 1) if row_count % count == 0)
    )
    blocks = row_count // group_rows
    shaped = tuple((member.reshape((blocks, group_rows) + member.shape[1:]) for member in arrays))
    results = lax.map(lambda pieces: kernel(*pieces), shaped)
    return jax.tree.map(lambda member: member.reshape((row_count,) + member.shape[2:]), results)


def attend_block(queries, key_rows, value_rows, allowed):
    scores = jnp.einsum("rqhd,rkhd->rhqk", queries, key_rows, preferred_element_type=jnp.float32)
    scores = jnp.where(allowed[:, None], scores, NEG_FILL)
    peak_score = jnp.max(scores, -1, keepdims=True)
    weights = jnp.exp(scores - peak_score)
    totals = jnp.sum(weights, -1, keepdims=True)
    prob_low = (weights / totals).astype(jnp.bfloat16)
    output = jnp.einsum("rhqk,rkhd->rqhd", prob_low, value_rows, preferred_element_type=jnp.float32)
    return (output, (peak_score + jnp.log(totals))[..., 0])


def attend_back(queries, key_rows, value_rows, allowed, log_total, grad_rows):
    scores = jnp.einsum("rqhd,rkhd->rhqk", queries, key_rows, preferred_element_type=jnp.float32)
    scores = jnp.where(allowed[:, None], scores, NEG_FILL)
    prob_full = jnp.exp(scores - log_total[..., None])
    prob_low = prob_full.astype(jnp.bfloat16)
    value_grad = jnp.einsum(
        "rhqk,rqhd->rkhd", prob_low, grad_rows, preferred_element_type=jnp.float32
    )
    prob_grad = jnp.einsum(
        "rqhd,rkhd->rhqk", grad_rows, value_rows, preferred_element_type=jnp.float32
    )
    offset = jnp.sum(prob_full * prob_grad, -1, keepdims=True)
    score_grad = (prob_full * (prob_grad - offset)).astype(jnp.bfloat16)
    query_grad = jnp.einsum(
        "rhqk,rkhd->rqhd", score_grad, key_rows, preferred_element_type=jnp.float32
    )
    key_grad = jnp.einsum(
        "rhqk,rqhd->rkhd", score_grad, queries, preferred_element_type=jnp.float32
    )
    return (query_grad, key_grad, value_grad)


def body(
    hidden,
    memory,
    out_grad,
    dec_starts,
    dec_length,
    mem_starts,
    mem_length,
    self_qkv,
    self_qv_bias,
    self_proj,
    cross_query,
    cross_kv,
    cross_qv_bias,
    cross_proj,
    ffn_in,
    ffn_in_bias,
    ffn_out,
    out_biases,
    norm_gains,
    norm_biases,
):
    row_count = dec_starts.shape[0]
    dec_slots = hidden.shape[0] // row_count
    mem_slots = memory.shape[0] // row_count
    local_width = self_qkv.shape[2]
    head_count = local_width // HD
    scaling = HD ** (-0.5)
    dec_places = jnp.arange(dec_slots, dtype=jnp.int32)
    mem_places = jnp.arange(mem_slots, dtype=jnp.int32)
    dec_segment = segment_ids(dec_starts, dec_slots)
    mem_segment = segment_ids(mem_starts, mem_slots)
    self_allowed = (
        (dec_segment[:, :, None] == dec_segment[:, None, :])
        & (dec_places[None, None, :] <= dec_places[None, :, None])
        & (dec_places[None, None, :] < dec_length[:, None, None])
    )
    cross_allowed = (dec_segment[:, :, None] == mem_segment[:, None, :]) & (
        mem_places[None, None, :] < mem_length[:, None, None]
    )

    def split_heads(values):
        return values.reshape(row_count, values.shape[0] // row_count, head_count, HD)

    def merge_heads(values):
        return values.reshape(row_count * values.shape[1], local_width)

    self_weight = jnp.concatenate([self_qkv[0], self_qkv[1], self_qkv[2]], axis=1)
    projected = jnp.dot(hidden, self_weight, preferred_element_type=jnp.float32)
    self_q = split_heads(
        ((projected[:, :local_width] + self_qv_bias[0]) * scaling).astype(jnp.bfloat16)
    )
    self_k = split_heads(projected[:, local_width : 2 * local_width].astype(jnp.bfloat16))
    self_v = split_heads((projected[:, 2 * local_width :] + self_qv_bias[1]).astype(jnp.bfloat16))
    self_out, self_total = row_groups(attend_block, (self_q, self_k, self_v, self_allowed))
    self_low = merge_heads(self_out).astype(jnp.bfloat16)
    self_branch = lax.psum(jnp.dot(self_low, self_proj, preferred_element_type=jnp.float32), "mp")
    first, first_back = jax.vjp(
        layer_norm,
        hidden.astype(jnp.float32) + self_branch + out_biases[0],
        norm_gains[0],
        norm_biases[0],
    )
    first_low = first.astype(jnp.bfloat16)
    cross_pre = jnp.dot(first_low, cross_query, preferred_element_type=jnp.float32)
    cross_q = split_heads(((cross_pre + cross_qv_bias[0]) * scaling).astype(jnp.bfloat16))
    memory_whole = lax.all_gather(memory, "mp", axis=1, tiled=True)
    kv_weight = jnp.concatenate([cross_kv[0], cross_kv[1]], axis=1)
    memory_kv = jnp.dot(memory_whole, kv_weight, preferred_element_type=jnp.float32)
    cross_k = split_heads(memory_kv[:, :local_width].astype(jnp.bfloat16))
    cross_v = split_heads((memory_kv[:, local_width:] + cross_qv_bias[1]).astype(jnp.bfloat16))
    cross_out, cross_total = row_groups(attend_block, (cross_q, cross_k, cross_v, cross_allowed))
    cross_low = merge_heads(cross_out).astype(jnp.bfloat16)
    cross_branch = lax.psum(
        jnp.dot(cross_low, cross_proj, preferred_element_type=jnp.float32), "mp"
    )
    second, second_back = jax.vjp(
        layer_norm, first + cross_branch + out_biases[1], norm_gains[1], norm_biases[1]
    )
    second_low = second.astype(jnp.bfloat16)
    hidden_pre = jnp.dot(second_low, ffn_in, preferred_element_type=jnp.float32) + ffn_in_bias
    activated, gelu_back = jax.vjp(exact_gelu, hidden_pre)
    activated_low = activated.astype(jnp.bfloat16)
    ffn_branch = lax.psum(jnp.dot(activated_low, ffn_out, preferred_element_type=jnp.float32), "mp")
    final_norm, third_back = jax.vjp(
        layer_norm, second + ffn_branch + out_biases[2], norm_gains[2], norm_biases[2]
    )
    third_grad, gain_three, shift_three = third_back(out_grad.astype(jnp.float32))
    third_low = third_grad.astype(jnp.bfloat16)
    ffn_out_grad = inner_dot(activated_low, third_low)
    ffn_bias_out = jnp.sum(third_grad, 0)
    (pre_grad,) = gelu_back(outer_dot(third_low, ffn_out))
    ffn_in_bias_grad = jnp.sum(pre_grad, 0)
    pre_low = pre_grad.astype(jnp.bfloat16)
    ffn_in_grad = inner_dot(second_low, pre_low)
    second_grad = third_grad + lax.psum(outer_dot(pre_low, ffn_in), "mp")
    cross_grad, gain_two, shift_two = second_back(second_grad)
    cross_grad_low = cross_grad.astype(jnp.bfloat16)
    cross_proj_grad = inner_dot(cross_low, cross_grad_low)
    cross_bias_out = jnp.sum(cross_grad, 0)
    cross_out_grad = split_heads(outer_dot(cross_grad_low, cross_proj).astype(jnp.bfloat16))
    cq_grad, ck_grad, cv_grad = row_groups(
        attend_back, (cross_q, cross_k, cross_v, cross_allowed, cross_total, cross_out_grad)
    )
    cq_grad = merge_heads(cq_grad) * scaling
    cv_grad = merge_heads(cv_grad)
    cross_qv_grad = jnp.stack([jnp.sum(cq_grad, 0), jnp.sum(cv_grad, 0)])
    cq_low = cq_grad.astype(jnp.bfloat16)
    cross_query_grad = inner_dot(first_low, cq_low)
    first_grad = cross_grad + lax.psum(outer_dot(cq_low, cross_query), "mp")
    kv_grad_low = jnp.concatenate([merge_heads(ck_grad), cv_grad], axis=1).astype(jnp.bfloat16)
    kv_weight_grad = inner_dot(memory_whole, kv_grad_low)
    cross_kv_grad = jnp.stack([kv_weight_grad[:, :local_width], kv_weight_grad[:, local_width:]])
    memory_grad = lax.psum_scatter(
        outer_dot(kv_grad_low, kv_weight).astype(jnp.bfloat16),
        "mp",
        scatter_dimension=1,
        tiled=True,
    ).astype(jnp.float32)
    self_grad, gain_one, shift_one = first_back(first_grad)
    self_grad_low = self_grad.astype(jnp.bfloat16)
    self_proj_grad = inner_dot(self_low, self_grad_low)
    self_bias_out = jnp.sum(self_grad, 0)
    self_out_grad = split_heads(outer_dot(self_grad_low, self_proj).astype(jnp.bfloat16))
    sq_grad, sk_grad, sv_grad = row_groups(
        attend_back, (self_q, self_k, self_v, self_allowed, self_total, self_out_grad)
    )
    sq_grad = merge_heads(sq_grad) * scaling
    sv_grad = merge_heads(sv_grad)
    self_qv_grad = jnp.stack([jnp.sum(sq_grad, 0), jnp.sum(sv_grad, 0)])
    qkv_low = jnp.concatenate([sq_grad, merge_heads(sk_grad), sv_grad], axis=1).astype(jnp.bfloat16)
    qkv_weight_grad = inner_dot(hidden, qkv_low)
    self_qkv_grad = jnp.stack(
        [
            qkv_weight_grad[:, :local_width],
            qkv_weight_grad[:, local_width : 2 * local_width],
            qkv_weight_grad[:, 2 * local_width :],
        ]
    )
    hidden_grad = self_grad + lax.psum(
        outer_dot(qkv_low, self_weight).astype(jnp.bfloat16), "mp"
    ).astype(jnp.float32)
    (
        self_qkv_grad,
        self_qv_grad,
        self_proj_grad,
        cross_query_grad,
        cross_kv_grad,
        cross_qv_grad,
        cross_proj_grad,
        ffn_in_grad,
        ffn_in_bias_grad,
        ffn_out_grad,
        self_bias_out,
        cross_bias_out,
        ffn_bias_out,
        gain_one,
        gain_two,
        gain_three,
        shift_one,
        shift_two,
        shift_three,
    ) = lax.psum(
        (
            self_qkv_grad,
            self_qv_grad,
            self_proj_grad,
            cross_query_grad,
            cross_kv_grad,
            cross_qv_grad,
            cross_proj_grad,
            ffn_in_grad,
            ffn_in_bias_grad,
            ffn_out_grad,
            self_bias_out,
            cross_bias_out,
            ffn_bias_out,
            gain_one,
            gain_two,
            gain_three,
            shift_one,
            shift_two,
            shift_three,
        ),
        "dp",
    )
    out_biases_grad = jnp.stack([self_bias_out, cross_bias_out, ffn_bias_out])
    norm_gains_grad = jnp.stack([gain_one, gain_two, gain_three])
    norm_biases_grad = jnp.stack([shift_one, shift_two, shift_three])
    return (
        final_norm.astype(jnp.bfloat16),
        hidden_grad,
        memory_grad,
        self_qkv_grad,
        self_qv_grad,
        self_proj_grad,
        cross_query_grad,
        cross_kv_grad,
        cross_qv_grad,
        cross_proj_grad,
        ffn_in_grad,
        ffn_in_bias_grad,
        ffn_out_grad,
        out_biases_grad,
        norm_gains_grad,
        norm_biases_grad,
    )


def solution(mesh):
    placed = (
        P("dp", None),
        P("dp", "mp"),
        P("dp", None),
        P("dp", None),
        P("dp"),
        P("dp", None),
        P("dp"),
        P(None, None, "mp"),
        P(None, "mp"),
        P("mp", None),
        P(None, "mp"),
        P(None, None, "mp"),
        P(None, "mp"),
        P("mp", None),
        P(None, "mp"),
        P("mp"),
        P("mp", None),
        P(),
        P(),
        P(),
    )
    return jax.shard_map(
        body,
        mesh=mesh,
        in_specs=placed,
        out_specs=(
            P("dp", None),
            P("dp", None),
            P("dp", "mp"),
            P(None, None, "mp"),
            P(None, "mp"),
            P("mp", None),
            P(None, "mp"),
            P(None, None, "mp"),
            P(None, "mp"),
            P("mp", None),
            P(None, "mp"),
            P("mp"),
            P("mp", None),
            P(),
            P(),
            P(),
        ),
        check_vma=False,
    )
```

profile of v0, /device:TPU:0, one launch (start us, length us, event | category | flops | bytes accessed | tf_op | source)
XLA Modules:
  0.0 875.1 jit_solution(11104530872102401639)
XLA Ops:
  17.6 69.4 %all-reduce.10.cloned.1.call-done = f32[512,768]{1,0:T(8,128)} async-done(((f32[512,768]{1,0:T(8,128)}), f32[512,768]{1,0:T(8,128)}) %all-reduce.10.cloned.1.call-update) | async-done | bytes 1572880 | tf_op jit(solution)/shard_map/psum | solution.py:140
  92.5 110.5 %all-gather.2.cloned.1.call-done = bf16[4096,768]{0,1:T(8,128)(2,1)} async-done(((bf16[4096,192]{0,1:T(8,128)(2,1)}), bf16[4096,768]{0,1:T(8,128)(2,1)}) %all-gather.2.cloned.1.call-update) | async-done | bytes 6291472 | tf_op jit(solution)/shard_map/all_gather | solution.py:150
  203.0 4.8 convolution_bitcast_fusion
  211.8 3.9 squeeze.90
  215.7 3.4 fusion.4
  219.0 3.9 squeeze.88
  222.9 3.5 select_reduce_fusion
  233.8 67.3 %all-reduce.12.cloned.1.call-done = f32[512,768]{1,0:T(8,128)} async-done(((f32[512,768]{1,0:T(8,128)}), f32[512,768]{1,0:T(8,128)}) %all-reduce.12.cloned.1.call-update) | async-done | bytes 1572880 | tf_op jit(solution)/shard_map/psum | solution.py:157
  303.8 5.4 multiply_convert_fusion.1
  312.1 68.3 %all-reduce.14.cloned.1.call-done = f32[512,768]{1,0:T(8,128)} async-done(((f32[512,768]{1,0:T(8,128)}), f32[512,768]{1,0:T(8,128)}) %all-reduce.14.cloned.1.call-update) | async-done | bytes 1572880 | tf_op jit(solution)/shard_map/psum | solution.py:167
  391.6 68.2 %all-reduce.16.cloned.1.call-done = f32[512,768]{1,0:T(8,128)} async-done(((f32[512,768]{1,0:T(8,128)}), f32[512,768]{1,0:T(8,128)}) %all-reduce.16.cloned.1.call-update) | async-done | bytes 1572880 | tf_op jit(solution)/shard_map/psum | solution.py:179
  459.8 2.8 multiply_reduce_fusion.1
  465.0 6.5 multiply_reduce_fusion
  482.0 3.1 bitcast_convert_fusion
  489.5 56.1 %all-reduce.18.cloned.1.call-done = f32[512,768]{1,0:T(8,128)} async-done(((f32[512,768]{1,0:T(8,128)}), f32[512,768]{1,0:T(8,128)}) %all-reduce.18.cloned.1.call-update) | async-done | bytes 1572880 | tf_op jit(solution)/shard_map/psum | solution.py:193
  556.6 7.2 convolution_convert_fusion
  565.0 3.8 fusion.93
  571.2 5.5 convolution_bitcast_fusion.3
  587.4 10.8 %all-reduce.20.cloned.1.call-done = bf16[512,768]{1,0:T(8,128)(2,1)} async-done(((bf16[512,768]{1,0:T(8,128)(2,1)}), bf16[512,768]{1,0:T(8,128)(2,1)}) %all-reduce.20.cloned.1.call-update) | async-done | bytes 786448 | tf_op jit(solution)/shard_map/psum | solution.py:223
  600.8 25.6 %all-reduce = (f32[2,192]{1,0:T(2,128)}, f32[2,192]{1,0:T(2,128)}, f32[768]{0:T(1024)}, f32[1,768]{1,0:T(1,128)S(1)}, f32[1,768]{1,0:T(1,128)S(1)}, /*index=5*/f...) all-reduce(f32[2,192]{1,0:T(2,128)S(1)} %pad_maximum_fusion.11, ...), channel_id=1, replica_groups=mesh['dp'=8,'mp'=4] {'dp'}, use_global_device_ids=true, to_apply=%region_30.31 | all-reduce | flops 8448 | bytes 67584 | tf_op jit(solution)/shard_map/psum | solution.py:246
  628.2 82.3 %reduce-scatter.2.cloned.1.call-done = bf16[4096,192]{0,1:T(8,128)(2,1)} async-done(((bf16[4096,768]{0,1:T(8,128)(2,1)}), bf16[4096,192]{0,1:T(8,128)(2,1)}) %reduce-scatter.2.cloned.1.call-update) | async-done | bytes 1572880 | tf_op jit(solution)/shard_map/reduce_scatter | solution.py:197
  710.5 3.4 convert_element_type.157
  714.0 143.3 %all-reduce.22.cloned.1.call-done = (f32[3,768,192]{1,2,0:T(8,128)}, f32[192,768]{1,0:T(8,128)}, f32[768,192]{0,1:T(8,128)}, f32[2,768,192]{1,2,0:T(8,128)}, f32...) async-done(((f32[3,768,192]{1,2,0:T(8,128)}, f32[192,768]{1,0:T(8,128)}, f32[768,192]{0,1:T(8,128)}, f32[2,768,192]{1,2,0:T(8,128)}, f32[192,768]{1,0:T(8,128)}, ...) | async-done | bytes 9437200 | tf_op jit(solution)/shard_map/psum | solution.py:246
  857.3 2.9 copy.229
  (316 shorter events, 97.9 us)
Async XLA Ops:
  7.2 296.3 %copy-start = (bf16[768,768]{1,0:T(8,128)(2,1)S(1)}, bf16[768,768]{1,0:T(8,128)(2,1)}, u32[]{:S(2)}) copy-start(bf16[768,768]{1,0:T(8,128)(2,1)} %param.34) | copy-start | bytes 3538948
  7.2 79.8 %all-reduce.10.cloned.1.call-start = ((), (), s32[]{:S(2)}) async-start(), calls=%async_computation.1 | async-start | bytes 3145728 | tf_op jit(solution)/shard_map/psum | solution.py:140
  15.0 188.0 %all-gather.2.cloned.1.call-start = ((), (), s32[]{:S(2)}) async-start(), calls=%async_computation.2 | async-start | bytes 7864320 | tf_op jit(solution)/shard_map/all_gather | solution.py:150
  15.8 285.3 %all-reduce.12.cloned.1.call-start = ((), (), s32[]{:S(2)}) async-start(), calls=%async_computation.3 | async-start | bytes 3145728 | tf_op jit(solution)/shard_map/psum | solution.py:157
  16.1 364.2 %copy-start.63 = (f32[768]{0:T(1024)}, f32[768]{0:T(1024)S(1)}, u32[]{:S(2)}) copy-start(f32[768]{0:T(1024)S(1)} %get-tuple-element.122) | copy-start | bytes 9220
  16.7 211.4 %copy-start.12 = (pred[4,128,1024]{2,1,0:T(8,128)(4,1)}, pred[4,128,1024]{2,1,0:T(8,128)(4,1)S(1)}, u32[]{:S(2)}) copy-start(pred[4,128,1024]{2,1,0:T(8,128)(4,1)S(1)} %compare_and_fusion) | copy-start | bytes 1572868
  88.9 212.2 %copy-start.3 = (f32[512,768]{1,0:T(8,128)}, f32[512,768]{1,0:T(8,128)S(1)}, u32[]{:S(2)}) copy-start(f32[512,768]{1,0:T(8,128)S(1)} %get-tuple-element.170) | copy-start | bytes 4718596
  233.6 146.7 %all-reduce.14.cloned.1.call-start = ((), (), s32[]{:S(2)}) async-start(), calls=%async_computation.4 | async-start | bytes 3145728 | tf_op jit(solution)/shard_map/psum | solution.py:167
  303.1 6.1 copy-start.5
  303.8 6.3 copy-start.74
  312.0 68.3 %copy-start.6 = (f32[512,768]{1,0:T(8,128)S(1)}, f32[512,768]{1,0:T(8,128)}, u32[]{:S(2)}) copy-start(f32[512,768]{1,0:T(8,128)} %copy-done.5) | copy-start | bytes 4718596
  312.0 147.8 %all-reduce.16.cloned.1.call-start = ((), (), s32[]{:S(2)}) async-start(), calls=%async_computation.5 | async-start | bytes 3145728 | tf_op jit(solution)/shard_map/psum | solution.py:179
  391.5 154.1 %all-reduce.18.cloned.1.call-start = ((), (), s32[]{:S(2)}) async-start(), calls=%async_computation.6 | async-start | bytes 3145728 | tf_op jit(solution)/shard_map/psum | solution.py:193
  465.0 6.5 slice-start
  465.0 6.5 slice-start.1
  477.2 4.8 slice-start.2
  477.2 121.0 %all-reduce.20.cloned.1.call-start = ((), (), s32[]{:S(2)}) async-start(), calls=%async_computation.7 | async-start | bytes 1572864 | tf_op jit(solution)/shard_map/psum | solution.py:223
  477.5 4.5 slice-start.3
  488.2 57.4 %copy-start.4 = (f32[512,768]{1,0:T(8,128)S(1)}, f32[512,768]{1,0:T(8,128)}, u32[]{:S(2)}) copy-start(f32[512,768]{1,0:T(8,128)} %copy-done.3) | copy-start | bytes 4718596
  555.3 155.2 %reduce-scatter.2.cloned.1.call-start = ((), (), s32[]{:S(2)}) async-start(), calls=%async_computation.8 | async-start | bytes 7864320 | tf_op jit(solution)/shard_map/reduce_scatter | solution.py:197
  563.9 4.9 copy-start.7
  563.9 4.9 copy-start.64
  563.9 293.4 %all-reduce.22.cloned.1.call-start = ((), (), s32[]{:S(2)}) async-start(), calls=%async_computation.9 | async-start | bytes 18874368 | tf_op jit(solution)/shard_map/psum | solution.py:246
  587.4 13.4 %copy-start.68 = (f32[768]{0:T(1024)S(1)}, f32[768]{0:T(1024)}, u32[]{:S(2)}) copy-start(f32[768]{0:T(1024)} %get-tuple-element.210) | copy-start | bytes 9220
  (71 other events, 118.6 us)
Sparse Core Ops, SparseCore 0:
  15.2 71.7 all-reduce.9
  88.6 114.3 all-gather.1
  233.7 67.3 all-reduce.11
  312.2 68.1 all-reduce.13
  391.6 68.1 all-reduce.15
  477.4 68.1 all-reduce.17
  555.4 42.7 all-reduce.19
  600.5 109.9 reduce-scatter.1
  716.5 140.7 all-reduce.21
where the time goes:
time: 884 us; the launch traced here: 875 us
  waiting for transfers between devices  677 us (77%)
  matrix products  70.8 us (8%)
  local copies, waits for them, and re-layouts  47.4 us (5%)
  other arithmetic  37.7 us (4%)
  blocking collectives  25.6 us (3%)
  between operations  15.5 us (2%)
    psum x1, waiting for transfers between devices, body(): lax.psum((self_qkv_grad, self_qv_grad, self_proj_grad, cross_query_grad,...  143 us
    all_gather x1, waiting for transfers between devices, body(): memory_whole = lax.all_gather(memory, 'mp', axis=1, tiled=True)  110 us
    reduce_scatter x1, waiting for transfers between devices, body(): lax.psum_scatter(outer_dot(kv_grad_low, kv_weight).astype(jnp.bfloat16),...  82.3 us
    psum x1, waiting for transfers between devices, body(): lax.psum(jnp.dot(self_low, self_proj, preferred_element_type=jnp.float32)...  69.4 us
    psum x1, waiting for transfers between devices, body(): lax.psum(jnp.dot(activated_low, ffn_out, preferred_element_type=jnp.float...  68.3 us
    psum x1, waiting for transfers between devices, body(): second_grad = third_grad + lax.psum(outer_dot(pre_low, ffn_in), 'mp')  68.2 us
    psum x1, waiting for transfers between devices, body(): lax.psum(jnp.dot(cross_low, cross_proj, preferred_element_type=jnp.float3...  67.3 us
    psum x1, waiting for transfers between devices, body(): first_grad = cross_grad + lax.psum(outer_dot(cq_low, cross_query), 'mp')  56.1 us
  transfers between devices with their start and end apart: 9, of which 9 were waited for; matrix products, arithmetic and copies ran while one was open for 6% of the time, Pallas kernels for 0%

commit v1 on v0

--- a/solution.py
+++ b/solution.py
@@ -147,7 +147,12 @@
     first_low = first.astype(jnp.bfloat16)
     cross_pre = jnp.dot(first_low, cross_query, preferred_element_type=jnp.float32)
     cross_q = split_heads(((cross_pre + cross_qv_bias[0]) * scaling).astype(jnp.bfloat16))
-    memory_whole = lax.all_gather(memory, "mp", axis=1, tiled=True)
+    ring = [memory]
+    for hop in range(3):
+        ring.append(lax.ppermute(ring[-1], "mp", [(dev, (dev + 1) % 4) for dev in range(4)]))
+    memory_whole = jnp.roll(
+        jnp.concatenate(ring[::-1], axis=1), (lax.axis_index("mp") + 1) * ring[0].shape[1], axis=1
+    )
     kv_weight = jnp.concatenate([cross_kv[0], cross_kv[1]], axis=1)
     memory_kv = jnp.dot(memory_whole, kv_weight, preferred_element_type=jnp.float32)
     cross_k = split_heads(memory_kv[:, :local_width].astype(jnp.bfloat16))

time: 884 us -> 858 us (0.971)
  waiting for transfers between devices: 677 us -> 642 us
  local copies, waits for them, and re-layouts: 47.4 us -> 59.2 us
    all_gather x1 -> x0, waiting for transfers between devices: 110 us -> none  [body(): memory_whole = lax.all_gather(memory, 'mp', axis=1, tiled=True)]
    ppermute x0 -> x3, waiting for transfers between devices: none -> 89.7 us  [body(): lax.ppermute(ring[-1], 'mp', [(dev, (dev + 1) % 4) for dev in range(4)])]
    psum x1, waiting for transfers between devices: 69.4 us -> 57.2 us  [body(): lax.psum(jnp.dot(self_low, self_proj, preferred_element_type=jnp.float32)...]
    unnamed x184 -> x211, local copies, waits for them, and re-layouts: 29.7 us -> 39.6 us
  transfers between devices with their start and end apart: 9 -> 11, of which waited for: 9 -> 10; matrix products, arithmetic and copies ran while one was open for 6% -> 7% of each run, Pallas kernels for 0% -> 0%
where the time goes in v1:
time: 858 us; the launch traced here: 854 us
  waiting for transfers between devices  642 us (75%)
  matrix products  68.8 us (8%)
  local copies, waits for them, and re-layouts  59.2 us (7%)
  other arithmetic  37.4 us (4%)
  blocking collectives  25.3 us (3%)
  between operations  16 us (2%)
    psum x1, waiting for transfers between devices, body(): lax.psum((self_qkv_grad, self_qv_grad, self_proj_grad, cross_query_grad,...  143 us
    ppermute x3, waiting for transfers between devices, body(): lax.ppermute(ring[-1], 'mp', [(dev, (dev + 1) % 4) for dev in range(4)])  89.7 us
    reduce_scatter x1, waiting for transfers between devices, body(): lax.psum_scatter(outer_dot(kv_grad_low, kv_weight).astype(jnp.bfloat16),...  82.8 us
    psum x1, waiting for transfers between devices, body(): lax.psum(jnp.dot(activated_low, ffn_out, preferred_element_type=jnp.float...  68.3 us
    psum x1, waiting for transfers between devices, body(): second_grad = third_grad + lax.psum(outer_dot(pre_low, ffn_in), 'mp')  68 us
    psum x1, waiting for transfers between devices, body(): lax.psum(jnp.dot(cross_low, cross_proj, preferred_element_type=jnp.float3...  66.5 us
    psum x1, waiting for transfers between devices, body(): lax.psum(jnp.dot(self_low, self_proj, preferred_element_type=jnp.float32)...  57.2 us
    psum x1, waiting for transfers between devices, body(): first_grad = cross_grad + lax.psum(outer_dot(cq_low, cross_query), 'mp')  56 us
  transfers between devices with their start and end apart: 11, of which 10 were waited for; matrix products, arithmetic and copies ran while one was open for 7% of the time, Pallas kernels for 0%

profile of v1, /device:TPU:0, one launch (start us, length us, event | category | flops | bytes accessed | tf_op | source)
XLA Modules:
  0.0 853.5 jit_solution(17289624148021000973)
XLA Ops:
  7.3 3.1 collective-permute-start
  14.9 32.1 %collective-permute-done = bf16[4096,192]{0,1:T(8,128)(2,1)S(1)} collective-permute-done((bf16[4096,192]{0,1:T(8,128)(2,1)}, bf16[4096,192]{0,1:T(8,128)(2,1)S(1)}, u32[]{:S(2)}, u32[]{:S(2)}) %collective-permute-start) | collective-permute-done | bytes 1572896 | tf_op jit(solution)/shard_map/ppermute | solution.py:152
  52.2 57.7 %collective-permute-done.1 = bf16[4096,192]{0,1:T(8,128)(2,1)} collective-permute-done((bf16[4096,192]{0,1:T(8,128)(2,1)S(1)}, bf16[4096,192]{0,1:T(8,128)(2,1)}, u32[]{:S(2)}, u32[]{:S(2)}) %collective-permute-start.1) | collective-permute-done | bytes 1572896 | tf_op jit(solution)/shard_map/ppermute | solution.py:152
  110.4 57.2 %all-reduce.10.cloned.1.call-done = f32[512,768]{1,0:T(8,128)} async-done(((f32[512,768]{1,0:T(8,128)}), f32[512,768]{1,0:T(8,128)}) %all-reduce.10.cloned.1.call-update) | async-done | bytes 1572880 | tf_op jit(solution)/shard_map/psum | solution.py:140
  190.0 3.9 squeeze.90
  193.8 3.4 fusion.8
  197.2 3.9 squeeze.88
  201.0 3.5 select_reduce_fusion
  212.0 66.5 %all-reduce.12.cloned.1.call-done = f32[512,768]{1,0:T(8,128)} async-done(((f32[512,768]{1,0:T(8,128)}), f32[512,768]{1,0:T(8,128)}) %all-reduce.12.cloned.1.call-update) | async-done | bytes 1572880 | tf_op jit(solution)/shard_map/psum | solution.py:162
  281.2 5.4 multiply_convert_fusion.1
  289.5 68.3 %all-reduce.14.cloned.1.call-done = f32[512,768]{1,0:T(8,128)} async-done(((f32[512,768]{1,0:T(8,128)}), f32[512,768]{1,0:T(8,128)}) %all-reduce.14.cloned.1.call-update) | async-done | bytes 1572880 | tf_op jit(solution)/shard_map/psum | solution.py:172
  369.7 68.0 %all-reduce.16.cloned.1.call-done = f32[512,768]{1,0:T(8,128)} async-done(((f32[512,768]{1,0:T(8,128)}), f32[512,768]{1,0:T(8,128)}) %all-reduce.16.cloned.1.call-update) | async-done | bytes 1572880 | tf_op jit(solution)/shard_map/psum | solution.py:184
  443.0 6.5 multiply_reduce_fusion
  460.0 3.2 bitcast_convert_fusion
  467.5 56.0 %all-reduce.18.cloned.1.call-done = f32[512,768]{1,0:T(8,128)} async-done(((f32[512,768]{1,0:T(8,128)}), f32[512,768]{1,0:T(8,128)}) %all-reduce.18.cloned.1.call-update) | async-done | bytes 1572880 | tf_op jit(solution)/shard_map/psum | solution.py:198
  534.6 7.2 convolution_convert_fusion
  543.0 3.8 fusion.99
  549.2 5.5 fusion.1
  566.1 10.1 %all-reduce.20.cloned.1.call-done = bf16[512,768]{1,0:T(8,128)(2,1)} async-done(((bf16[512,768]{1,0:T(8,128)(2,1)}), bf16[512,768]{1,0:T(8,128)(2,1)}) %all-reduce.20.cloned.1.call-update) | async-done | bytes 786448 | tf_op jit(solution)/shard_map/psum | solution.py:228
  578.7 25.3 %all-reduce = (f32[2,192]{1,0:T(2,128)}, f32[2,192]{1,0:T(2,128)}, f32[768]{0:T(1024)}, f32[1,768]{1,0:T(1,128)S(1)}, f32[1,768]{1,0:T(1,128)S(1)}, /*index=5*/f...) all-reduce(f32[2,192]{1,0:T(2,128)S(1)} %pad_maximum_fusion.11, ...), channel_id=1, replica_groups=mesh['dp'=8,'mp'=4] {'dp'}, use_global_device_ids=true, to_apply=%region_30.31 | all-reduce | flops 8448 | bytes 67584 | tf_op jit(solution)/shard_map/psum | solution.py:251
  605.8 82.8 %reduce-scatter.2.cloned.1.call-done = bf16[4096,192]{0,1:T(8,128)(2,1)} async-done(((bf16[4096,768]{0,1:T(8,128)(2,1)}), bf16[4096,192]{0,1:T(8,128)(2,1)}) %reduce-scatter.2.cloned.1.call-update) | async-done | bytes 1572880 | tf_op jit(solution)/shard_map/reduce_scatter | solution.py:202
  688.6 3.4 convert_element_type.157
  692.0 143.3 %all-reduce.22.cloned.1.call-done = (f32[3,768,192]{1,2,0:T(8,128)}, f32[192,768]{1,0:T(8,128)}, f32[768,192]{0,1:T(8,128)}, f32[2,768,192]{1,2,0:T(8,128)}, f32...) async-done(((f32[3,768,192]{1,2,0:T(8,128)}, f32[192,768]{1,0:T(8,128)}, f32[768,192]{0,1:T(8,128)}, f32[2,768,192]{1,2,0:T(8,128)}, f32[192,768]{1,0:T(8,128)}, ...) | async-done | bytes 9437200 | tf_op jit(solution)/shard_map/psum | solution.py:251
  835.4 2.9 copy.236
  (347 shorter events, 114.8 us)
Async XLA Ops:
  7.2 273.7 %copy-start = (bf16[768,768]{1,0:T(8,128)(2,1)S(1)}, bf16[768,768]{1,0:T(8,128)(2,1)}, u32[]{:S(2)}) copy-start(bf16[768,768]{1,0:T(8,128)(2,1)} %param.34) | copy-start | bytes 3538948
  7.2 160.4 %all-reduce.10.cloned.1.call-start = ((), (), s32[]{:S(2)}) async-start(), calls=%async_computation.1 | async-start | bytes 3145728 | tf_op jit(solution)/shard_map/psum | solution.py:140
  7.3 39.7 %collective-permute-start = (bf16[4096,192]{0,1:T(8,128)(2,1)}, bf16[4096,192]{0,1:T(8,128)(2,1)S(1)}, u32[]{:S(2)}, u32[]{:S(2)}) collective-permute-start(bf16[4096,192]{0,1:T(8,128)(2,1)} %param.21), channel_id=1, source_target_pairs={{0,1},{1,2},{2,3},{3,0},{4,5},{5,6},{6,7},{7,4},{8,9},{9,10},{10,1... | collective-permute-start | bytes 4718600 | tf_op jit(solution)/shard_map/ppermute | solution.py:152
  14.0 33.0 %copy-start.44 = (bf16[192,768]{1,0:T(8,128)(2,1)S(1)}, bf16[192,768]{1,0:T(8,128)(2,1)}, u32[]{:S(2)}) copy-start(bf16[192,768]{1,0:T(8,128)(2,1)} %param.29) | copy-start | bytes 884740
  14.9 32.1 %copy-start.38 = (bf16[4,128,3,64]{1,0,3,2:T(4,128)(2,1)}, bf16[4,128,3,64]{1,0,3,2:T(4,128)(2,1)S(1)}, u32[]{:S(2)}) copy-start(bf16[4,128,3,64]{1,0,3,2:T(4,128)(2,1)S(1)} %copy.88) | copy-start | bytes 589828
  47.0 62.9 %collective-permute-start.1 = (bf16[4096,192]{0,1:T(8,128)(2,1)S(1)}, bf16[4096,192]{0,1:T(8,128)(2,1)}, u32[]{:S(2)}, u32[]{:S(2)}) collective-permute-start(bf16[4096,192]{0,1:T(8,128)(2,1)S(1)} %collective-permute-done), channel_id=1, source_target_pairs={{0,1},{1,2},{2,3},{3,0},{4,5},{5,6},{6,7},{7,4},{8,9},{9,10},{10,1... | collective-permute-start | bytes 4718600 | tf_op jit(solution)/shard_map/ppermute | solution.py:152
  48.6 61.7 %copy-start.76 = (f32[3,768]{1,0:T(4,128)S(1)}, f32[3,768]{1,0:T(4,128)}, u32[]{:S(2)}) copy-start(f32[3,768]{1,0:T(4,128)} %param.37) | copy-start | bytes 27652
  48.7 229.8 %all-reduce.12.cloned.1.call-start = ((), (), s32[]{:S(2)}) async-start(), calls=%async_computation.2 | async-start | bytes 3145728 | tf_op jit(solution)/shard_map/psum | solution.py:162
  50.1 156.1 %copy-start.12 = (pred[4,128,1024]{2,1,0:T(8,128)(4,1)}, pred[4,128,1024]{2,1,0:T(8,128)(4,1)S(1)}, u32[]{:S(2)}) copy-start(pred[4,128,1024]{2,1,0:T(8,128)(4,1)S(1)} %compare_and_fusion) | copy-start | bytes 1572868
  109.8 63.3 %collective-permute-start.2 = (bf16[4096,192]{0,1:T(8,128)(2,1)}, bf16[4096,192]{0,1:T(8,128)(2,1)}, u32[]{:S(2)}, u32[]{:S(2)}) collective-permute-start(bf16[4096,192]{0,1:T(8,128)(2,1)} %collective-permute-done.1), channel_id=1, source_target_pairs={{0,1},{1,2},{2,3},{3,0},{4,5},{5,6},{6,7},{7,4},{8,9},{9,10},{10,1... | collective-permute-start | bytes 4718600 | tf_op jit(solution)/shard_map/ppermute | solution.py:152
  169.5 109.0 %copy-start.3 = (f32[512,768]{1,0:T(8,128)}, f32[512,768]{1,0:T(8,128)S(1)}, u32[]{:S(2)}) copy-start(f32[512,768]{1,0:T(8,128)S(1)} %get-tuple-element.170) | copy-start | bytes 4718596
  211.7 146.1 %all-reduce.14.cloned.1.call-start = ((), (), s32[]{:S(2)}) async-start(), calls=%async_computation.3 | async-start | bytes 3145728 | tf_op jit(solution)/shard_map/psum | solution.py:172
  280.5 6.2 copy-start.5
  281.2 6.3 copy-start.84
  289.5 68.4 %copy-start.6 = (f32[512,768]{1,0:T(8,128)S(1)}, f32[512,768]{1,0:T(8,128)}, u32[]{:S(2)}) copy-start(f32[512,768]{1,0:T(8,128)} %copy-done.5) | copy-start | bytes 4718596
  289.5 148.2 %all-reduce.16.cloned.1.call-start = ((), (), s32[]{:S(2)}) async-start(), calls=%async_computation.4 | async-start | bytes 3145728 | tf_op jit(solution)/shard_map/psum | solution.py:184
  369.4 154.1 %all-reduce.18.cloned.1.call-start = ((), (), s32[]{:S(2)}) async-start(), calls=%async_computation.5 | async-start | bytes 3145728 | tf_op jit(solution)/shard_map/psum | solution.py:198
  442.9 6.5 slice-start
  443.0 6.5 slice-start.1
  455.2 120.9 %all-reduce.20.cloned.1.call-start = ((), (), s32[]{:S(2)}) async-start(), calls=%async_computation.6 | async-start | bytes 1572864 | tf_op jit(solution)/shard_map/psum | solution.py:228
  466.2 57.3 %copy-start.4 = (f32[512,768]{1,0:T(8,128)S(1)}, f32[512,768]{1,0:T(8,128)}, u32[]{:S(2)}) copy-start(f32[512,768]{1,0:T(8,128)} %copy-done.3) | copy-start | bytes 4718596
  533.3 155.3 %reduce-scatter.2.cloned.1.call-start = ((), (), s32[]{:S(2)}) async-start(), calls=%async_computation.7 | async-start | bytes 7864320 | tf_op jit(solution)/shard_map/reduce_scatter | solution.py:202
  541.9 293.5 %all-reduce.22.cloned.1.call-start = ((), (), s32[]{:S(2)}) async-start(), calls=%async_computation.8 | async-start | bytes 18874368 | tf_op jit(solution)/shard_map/psum | solution.py:251
  566.0 12.6 %copy-start.77 = (f32[768]{0:T(1024)S(1)}, f32[768]{0:T(1024)}, u32[]{:S(2)}) copy-start(f32[768]{0:T(1024)} %get-tuple-element.210) | copy-start | bytes 9220
  (83 other events, 163.9 us)
Sparse Core Ops, SparseCore 0:
  48.8 118.7 all-reduce.9
  211.8 66.6 all-reduce.11
  289.6 68.1 all-reduce.13
  369.5 68.1 all-reduce.15
  455.3 68.1 all-reduce.17
  533.4 42.7 all-reduce.19
  578.4 110.1 reduce-scatter.1
  694.5 140.7 all-reduce.21
